TPU v7x, 128 devices: a whole 4x4x4 slice. The times are simulated.
128 devices in a mesh: row: 16 (over y, z), col: 8 (over x, core).
Axes of the slice: x: 4, y: 4, z: 4, core: 2. Of those that a mesh axis runs over, the one named last changes fastest.
Arguments:
- descriptors: bfloat16 [131072, 512], P(('row', 'col')), may hold values from -6 to 6
- center_index: int32 [16384], replicated, may hold values from 0 to 131071, as said below
- panel_index: int32 [1], replicated, may hold values from 0 to 15
Outputs:
- schur: float32 [16384, 16384], P('row', 'col')
- panel_factor: float32 [16384, 1024], P('row', 'col')
Inputs may be any that keep to these rules, and one draw needn't show every extreme that they name: Center j is row center_index[j] mod 1024 of shard center_index[j] // 1024, shards numbered row-major over row and col. In each aligned run of 128 centers no shard supplies more than 4 centers, and some shard supplies exactly 4.
All inputs are finite; a program needn't handle non-finite values.
Results may differ from a plain program's by a relative error of at most 0.0003.
Values may be sent and summed in bfloat16 or wider, within the bound.
No kernel may reach another device: no remote copies, remote signals or barrier semaphores. Data moves between devices by JAX's collectives and lax.ppermute only.
A program may use at most 128 MiB of HBM per device.

v0:
```python
import jax
import jax.numpy as jnp
from jax import lax
from jax.sharding import PartitionSpec as P

D = 512
PANEL = 1024
GROUP = 128


ridge = 1.0


def broadcast(block, axis, holder):
    block = jnp.where(lax.axis_index(axis) == holder, block, jnp.zeros_like(block))
    return lax.psum(block, axis)


def gram_block(left, right, left_sq, right_sq):
    inner = lax.dot_general(
        left, right, (((1,), (1,)), ((), ())), preferred_element_type=jnp.float32
    )
    return jnp.exp(-(left_sq[:, None] + right_sq[None, :] - 2.0 * inner) / D)


def squares(values):
    return jnp.sum(jnp.square(values.astype(jnp.float32)), axis=1)


def transposed_product(left, right):
    return lax.dot_general(
        left,
        right,
        (((1,), (1,)), ((), ())),
        precision=lax.Precision.HIGHEST,
        preferred_element_type=jnp.float32,
    )


def body(descriptors, center_index, panel_index):
    rows_axis = lax.axis_size("row")
    cols_axis = lax.axis_size("col")
    device_count = rows_axis * cols_axis
    my_row = lax.axis_index("row")
    my_col = lax.axis_index("col")
    my_flat = my_row * cols_axis + my_col
    data_rows = descriptors.shape[0]
    capacity = max(4, 2 * GROUP // device_count)
    tile_rows = GROUP * cols_axis
    by_group = center_index.reshape(device_count, GROUP)
    shard_of = by_group // data_rows
    same_shard = shard_of[:, :, None] == shard_of[:, None, :]
    earlier = (
        jnp.arange(GROUP, dtype=jnp.int32)[None, :] < jnp.arange(GROUP, dtype=jnp.int32)[:, None]
    )
    slot_rank = jnp.sum((same_shard & earlier[None, :, :]).astype(jnp.int32), axis=2)
    targets = jnp.where(
        shard_of == my_flat,
        jnp.arange(device_count, dtype=jnp.int32)[:, None] * capacity + slot_rank,
        device_count * capacity,
    )
    local_row = by_group - my_flat * data_rows
    slot_rows = (
        jnp.zeros((device_count * capacity,), jnp.int32)
        .at[targets.reshape(-1)]
        .set(local_row.reshape(-1), mode="drop")
    )
    outgoing = jnp.take(descriptors, slot_rows, axis=0)
    arrived = lax.all_to_all(
        outgoing.reshape(device_count, capacity, D),
        ("row", "col"),
        split_axis=0,
        concat_axis=0,
        tiled=True,
    )
    my_shards = lax.dynamic_index_in_dim(shard_of, my_flat, 0, keepdims=False)
    my_ranks = lax.dynamic_index_in_dim(slot_rank, my_flat, 0, keepdims=False)
    my_centers = arrived[my_shards, my_ranks]
    row_centers = lax.all_gather(my_centers, "col", axis=0, tiled=True)
    col_centers = lax.all_gather(my_centers, "row", axis=0, tiled=True)
    row_sq = squares(row_centers)
    col_sq = squares(col_centers)
    row_pos = my_row * tile_rows + jnp.arange(tile_rows, dtype=jnp.int32)
    col_pos = (
        (jnp.arange(rows_axis, dtype=jnp.int32)[:, None] * cols_axis + my_col) * GROUP
        + jnp.arange(GROUP, dtype=jnp.int32)[None, :]
    ).reshape(-1)
    tile = gram_block(row_centers, col_centers, row_sq, col_sq)
    tile = tile + ridge * (row_pos[:, None] == col_pos[None, :]).astype(jnp.float32)
    start_pos = panel_index[0] * PANEL
    first_pos = start_pos + 0
    owner_row = first_pos // tile_rows
    pieces = broadcast(row_centers, "row", owner_row)
    panel_sq = squares(pieces)
    panel_pos = start_pos + jnp.arange(PANEL, dtype=jnp.int32)
    diag_block = gram_block(pieces, pieces, panel_sq, panel_sq) + ridge * jnp.eye(
        PANEL, dtype=jnp.float32
    )
    diag_factor = jnp.linalg.cholesky(diag_block)
    row_block = gram_block(row_centers, pieces, row_sq, panel_sq)
    row_block = row_block + ridge * (row_pos[:, None] == panel_pos[None, :]).astype(jnp.float32)
    row_factor = lax.linalg.triangular_solve(
        diag_factor, row_block, left_side=False, lower=True, transpose_a=True
    )
    own_rows = lax.dynamic_slice_in_dim(row_factor, my_col * GROUP, GROUP, 0)
    schur = tile - transposed_product(
        row_factor, lax.all_gather(own_rows, "row", axis=0, tiled=True)
    )
    share = PANEL // cols_axis
    panel_factor = lax.dynamic_slice_in_dim(row_factor, my_col * share, share, 1)
    return (schur, panel_factor)


def solution(mesh):
    return jax.shard_map(
        body,
        mesh=mesh,
        in_specs=(P(("row", "col"), None), P(), P()),
        out_specs=(P("row", "col"), P("row", "col")),
        check_vma=False,
    )
```

profile of v0, /device:TPU:0, one launch (start us, length us, event | category | flops | bytes accessed | tf_op | source)
XLA Modules:
  0.0 700.6 jit_solution(14249034032198965943)
XLA Ops:
  8.2 5.1 convert_reduce_fusion
  14.3 60.3 %scatter_custom_fusion = s32[512]{0:T(512)S(1)} fusion(s32[16384]{0:T(1024)S(1)} %get-tuple-element.74, s32[16384]{0:T(1024)S(1)} %get-tuple-element.73, s32[]{:T(128)} %copy.83), kind=kCustom, calls=%fused_computation.197 | custom fusion | bytes 2052 | tf_op jit(solution)/shard_map/scatter | solution.py:66
  74.6 2.0 gather_fusion
  78.0 11.2 %all-to-all-start = ((bf16[128,4,512]{2,1,0:T(4,128)(2,1)}), bf16[128,4,512]{2,1,0:T(4,128)(2,1)S(1)}, u32[]{:S(2)}, u32[]{:S(2)}) async-start(bf16[128,4,512]{2,1,0:T(4,128)(2,1)} %broadcast_select_fusion.1), calls=%async_computation | async-start | bytes 1048576 | tf_op jit(solution)/shard_map/all_to_all | solution.py:69
  89.2 13.4 %all-to-all-done = bf16[128,4,512]{2,1,0:T(4,128)(2,1)S(1)} async-done(((bf16[128,4,512]{2,1,0:T(4,128)(2,1)}), bf16[128,4,512]{2,1,0:T(4,128)(2,1)S(1)}, u32[]{:S(2)}, u32[]{:S(2)}) %all-to-all-start) | async-done | bytes 524320 | tf_op jit(solution)/shard_map/all_to_all | solution.py:69
  102.7 2.0 gather_fusion.1
  105.4 18.7 %all-gather.4.cloned.1.call-done = bf16[1024,512]{1,0:T(8,128)(2,1)} async-done(((bf16[128,512]{1,0:T(8,128)(2,1)}), bf16[1024,512]{1,0:T(8,128)(2,1)}) %all-gather.4.cloned.1.call-update) | async-done | bytes 1048592 | tf_op jit(solution)/shard_map/all_gather | solution.py:79
  125.9 1.5 multiply_reduce_fusion.2
  127.4 87.8 %all-reduce.3.cloned.1.call-done = bf16[1024,512]{1,0:T(8,128)(2,1)} async-done(((bf16[1024,512]{1,0:T(8,128)(2,1)}), bf16[1024,512]{1,0:T(8,128)(2,1)}) %all-reduce.3.cloned.1.call-update) | async-done | bytes 1048592 | tf_op jit(solution)/shard_map/psum | solution.py:16
  215.2 1.5 multiply_reduce_fusion.1
  216.7 7.7 %broadcast_add_fusion = (f32[1024,1024]{0,1:T(8,128)}, f32[1024,1024]{0,1:T(8,128)}, f32[1024,1024]{1,0:T(8,128)}) fusion(f32[1024]{0:T(1024)S(1)} %multiply_reduce_fusion.1, bf16[1024,512]{1,0:T(8,128)(2,1)} %all-reduce.3.cloned.1.call-done), kind=kOutput, calls=%fused_computation.24 | convolution fusion | flops 1077936128 | bytes 13635584 | tf_op jit(solution)/shard_map/dot_general | solution.py:20
  224.4 5.4 copy.20
  229.8 5.4 copy.21
  235.1 6.0 add_multiply_fusion
  241.2 1.9 copy-done.2
  243.1 11.7 %cholesky.223 = f32[128,128]{1,0:T(8,128)S(1)} custom-call(f32[128,128]{1,0:T(8,128)S(1)} %cholesky.580), custom_call_target="Cholesky" | custom-call | tf_op jit(solution)/shard_map/jit(cholesky)/cholesky | solution.py:99
  254.9 2.5 cholesky.255
  257.4 9.8 %custom-call.62 = f32[1,128,128]{1,2,0:T(8,128)S(1)} custom-call(f32[1,128,128]{2,1,0:T(8,128)S(1)} %get-tuple-element.72), custom_call_target="InvertDiagBlocksLowerTriangular" | custom-call | tf_op jit(solution)/shard_map/jit(cholesky)/cholesky | solution.py:99
  267.2 2.3 constant_dynamic-update-slice_fusion.25
  269.5 1.5 convolution_subtract_fusion.5
  271.1 11.7 %cholesky.244 = f32[128,128]{1,0:T(8,128)S(1)} custom-call(f32[128,128]{1,0:T(8,128)S(1)} %cholesky.584), custom_call_target="Cholesky" | custom-call | tf_op jit(solution)/shard_map/jit(cholesky)/cholesky | solution.py:99
  283.4 10.0 %custom-call.63 = f32[1,128,128]{1,2,0:T(8,128)S(1)} custom-call(f32[1,128,128]{2,1,0:T(8,128)S(1)} %get-tuple-element.69), custom_call_target="InvertDiagBlocksLowerTriangular" | custom-call | tf_op jit(solution)/shard_map/jit(cholesky)/cholesky | solution.py:99
  293.4 1.2 convolution_dynamic-update-slice_fusion.1
  294.6 2.1 convolution_subtract_fusion.6
  296.7 11.7 %cholesky.468 = f32[128,128]{1,0:T(8,128)S(1)} custom-call(f32[128,128]{1,0:T(8,128)S(1)} %cholesky.589), custom_call_target="Cholesky" | custom-call | tf_op jit(solution)/shard_map/jit(cholesky)/cholesky | solution.py:99
  309.7 9.8 %custom-call.64 = f32[1,128,128]{1,2,0:T(8,128)S(1)} custom-call(f32[1,128,128]{2,1,0:T(8,128)S(1)} %get-tuple-element.66), custom_call_target="InvertDiagBlocksLowerTriangular" | custom-call | tf_op jit(solution)/shard_map/jit(cholesky)/cholesky | solution.py:99
  320.7 2.3 convolution_subtract_fusion.7
  323.1 12.1 %cholesky.487 = f32[128,128]{1,0:T(8,128)S(1)} custom-call(f32[128,128]{1,0:T(8,128)S(1)} %cholesky.594), custom_call_target="Cholesky" | custom-call | tf_op jit(solution)/shard_map/jit(cholesky)/cholesky | solution.py:99
  336.5 9.8 %custom-call.65 = f32[1,128,128]{1,2,0:T(8,128)S(1)} custom-call(f32[1,128,128]{2,1,0:T(8,128)S(1)} %get-tuple-element.63), custom_call_target="InvertDiagBlocksLowerTriangular" | custom-call | tf_op jit(solution)/shard_map/jit(cholesky)/cholesky | solution.py:99
  347.3 2.3 convolution_subtract_fusion.8
  349.7 11.7 %cholesky.506 = f32[128,128]{1,0:T(8,128)S(1)} custom-call(f32[128,128]{1,0:T(8,128)S(1)} %cholesky.599), custom_call_target="Cholesky" | custom-call | tf_op jit(solution)/shard_map/jit(cholesky)/cholesky | solution.py:99
  362.8 9.8 %custom-call.66 = f32[1,128,128]{1,2,0:T(8,128)S(1)} custom-call(f32[1,128,128]{2,1,0:T(8,128)S(1)} %get-tuple-element.60), custom_call_target="InvertDiagBlocksLowerTriangular" | custom-call | tf_op jit(solution)/shard_map/jit(cholesky)/cholesky | solution.py:99
  373.6 2.5 convolution_subtract_fusion.9
  376.1 11.7 %cholesky.526 = f32[128,128]{1,0:T(8,128)S(1)} custom-call(f32[128,128]{1,0:T(8,128)S(1)} %cholesky.604), custom_call_target="Cholesky" | custom-call | tf_op jit(solution)/shard_map/jit(cholesky)/cholesky | solution.py:99
  389.0 9.8 %custom-call.67 = f32[1,128,128]{1,2,0:T(8,128)S(1)} custom-call(f32[1,128,128]{2,1,0:T(8,128)S(1)} %get-tuple-element.57), custom_call_target="InvertDiagBlocksLowerTriangular" | custom-call | tf_op jit(solution)/shard_map/jit(cholesky)/cholesky | solution.py:99
  399.8 2.2 convolution_subtract_fusion.10
  401.9 11.7 %cholesky.546 = f32[128,128]{1,0:T(8,128)S(1)} custom-call(f32[128,128]{1,0:T(8,128)S(1)} %cholesky.609), custom_call_target="Cholesky" | custom-call | tf_op jit(solution)/shard_map/jit(cholesky)/cholesky | solution.py:99
  414.9 10.0 %custom-call.68 = f32[1,128,128]{1,2,0:T(8,128)S(1)} custom-call(f32[1,128,128]{2,1,0:T(8,128)S(1)} %get-tuple-element.54), custom_call_target="InvertDiagBlocksLowerTriangular" | custom-call | tf_op jit(solution)/shard_map/jit(cholesky)/cholesky | solution.py:99
  425.8 1.8 convolution_subtract_fusion.11
  427.6 11.7 %cholesky.564 = f32[128,128]{1,0:T(8,128)S(1)} custom-call(f32[128,128]{1,0:T(8,128)S(1)} %convolution_subtract_fusion.11), custom_call_target="Cholesky" | custom-call | tf_op jit(solution)/shard_map/jit(cholesky)/cholesky | solution.py:99
  446.2 5.0 select_select_fusion
  451.3 24.1 %while.1 = (s32[]{:T(128)}, f32[1024,1024]{1,0:T(8,128)}, s32[8,2]{0,1:T(2,128)S(1)}, f32[8,128,128]{2,1,0:T(8,128)S(1)}, s32[]{:T(128)}) while((s32[]{:T(128)}, f32[1024,1024]{1,0:T(8,128)}, s32[8,2]{0,1:T(2,128)S(1)}, f32[8,128,128]{2,1,0:T(8,128)S(1)}, s32[]{:T(128)}) %tuple.67), condition=%wide.while_cond, body=%wide.while_body.sunk | while | flops 2 | bytes 131181 | solution.py:102
  451.9 2.3 bitcast_dynamic-update-slice_fusion.2
  455.0 2.3 bitcast_dynamic-update-slice_fusion.2
  458.0 2.3 bitcast_dynamic-update-slice_fusion.2
  461.0 2.3 bitcast_dynamic-update-slice_fusion.2
  464.0 2.3 bitcast_dynamic-update-slice_fusion.2
  467.1 2.3 bitcast_dynamic-update-slice_fusion.2
  470.1 2.3 bitcast_dynamic-update-slice_fusion.2
  473.1 2.3 bitcast_dynamic-update-slice_fusion.2
  475.4 79.0 %custom-call.69 = f32[8,128,128]{1,2,0:T(8,128)S(1)} custom-call(f32[8,128,128]{2,1,0:T(8,128)S(1)} %get-tuple-element.9), custom_call_target="InvertDiagBlocksLowerTriangular" | custom-call | tf_op jit(solution)/shard_map/triangular_solve | solution.py:102
  554.4 1.8 convert_add_fusion
  556.9 1.5 convolution_subtract_fusion.4
  559.1 1.6 convolution_subtract_fusion
  561.5 2.1 fusion.15
  564.3 2.2 fusion.18
  567.2 2.7 convolution_subtract_fusion.2
  570.6 3.0 convolution_subtract_fusion.1
  574.3 3.3 convolution_subtract_fusion.3
  578.2 2.0 copy-done.6
  583.4 2.1 multiply_reduce_fusion
  585.4 72.5 %all-gather.8.cloned.1.call-done = f32[2048,1024]{0,1:T(8,128)} async-done(((f32[128,1024]{0,1:T(8,128)}), f32[2048,1024]{0,1:T(8,128)}) %all-gather.8.cloned.1.call-update) | async-done | bytes 8388624 | tf_op jit(solution)/shard_map/all_gather | solution.py:107
  657.9 29.8 %fusion.80 = f32[1024,2048]{1,0:T(8,128)S(1)} fusion(f32[1024,1024]{0,1:T(8,128)} %copy-done.6, f32[2048,1024]{0,1:T(8,128)} %all-gather.8.cloned.1.call-done), kind=kOutput, calls=%fused_computation.212 | convolution fusion | flops 25769803776 | bytes 20971520 | tf_op jit(solution)/shard_map/dot_general | solution.py:31
  687.8 6.1 add_subtract_fusion
  (94 shorter events, 33.3 us)
Async XLA Ops:
  7.2 67.4 %copy-start = (bf16[1024,512]{1,0:T(8,128)(2,1)S(1)}, bf16[1024,512]{1,0:T(8,128)(2,1)}, u32[]{:S(2)}) copy-start(bf16[1024,512]{1,0:T(8,128)(2,1)} %param.3) | copy-start | bytes 3145732
  78.0 24.7 %all-to-all-start = ((bf16[128,4,512]{2,1,0:T(4,128)(2,1)}), bf16[128,4,512]{2,1,0:T(4,128)(2,1)S(1)}, u32[]{:S(2)}, u32[]{:S(2)}) async-start(bf16[128,4,512]{2,1,0:T(4,128)(2,1)} %broadcast_select_fusion.1), calls=%async_computation | async-start | bytes 1048576 | tf_op jit(solution)/shard_map/all_to_all | solution.py:69
  89.2 34.9 %all-gather.4.cloned.1.call-start = ((), (), s32[]{:S(2)}) async-start(), calls=%async_computation.1 | async-start | bytes 1179648 | tf_op jit(solution)/shard_map/all_gather | solution.py:79
  104.6 110.6 %all-reduce.3.cloned.1.call-start = ((), (), s32[]{:S(2)}) async-start(), calls=%async_computation.3 | async-start | bytes 2097152 | tf_op jit(solution)/shard_map/psum | solution.py:16
  125.1 458.3 %all-gather.6.cloned.1.call-start = ((), (), s32[]{:S(2)}) async-start(), calls=%async_computation.2 | async-start | bytes 2228224 | tf_op jit(solution)/shard_map/all_gather | solution.py:80
  125.8 532.1 %all-gather.8.cloned.1.call-start = ((), (), s32[]{:S(2)}) async-start(), calls=%async_computation.4 | async-start | bytes 8912896 | tf_op jit(solution)/shard_map/all_gather | solution.py:107
  241.2 1.9 copy-start.2
  446.2 108.2 %copy-start.3 = (bf16[1024,512]{1,0:T(8,128)(2,1)S(1)}, bf16[1024,512]{1,0:T(8,128)(2,1)}, u32[]{:S(2)}) copy-start(bf16[1024,512]{1,0:T(8,128)(2,1)} %all-reduce.3.cloned.1.call-done) | copy-start | bytes 3145732
  446.2 108.2 %copy-start.4 = (bf16[1024,512]{1,0:T(8,128)(2,1)S(1)}, bf16[1024,512]{1,0:T(8,128)(2,1)}, u32[]{:S(2)}) copy-start(bf16[1024,512]{1,0:T(8,128)(2,1)} %all-gather.4.cloned.1.call-done) | copy-start | bytes 3145732
  578.2 2.0 copy-start.6
  657.9 29.8 %copy-start.5 = (bf16[2048,512]{1,0:T(8,128)(2,1)S(1)}, bf16[2048,512]{1,0:T(8,128)(2,1)}, u32[]{:S(2)}) copy-start(bf16[2048,512]{1,0:T(8,128)(2,1)} %all-gather.6.cloned.1.call-done) | copy-start | bytes 6291460
  687.8 6.1 copy-start.1
Sparse Core Ops, SparseCore 0:
  104.8 19.2 all-gather.3
  127.9 87.3 all-reduce.2
  217.4 44.5 all-gather.5
  581.3 76.5 all-gather.7
where the time goes:
time: 708 us; the launch traced here: 701 us
  other arithmetic  277 us (39%)
  waiting for transfers between devices  193 us (27%)
  local copies, waits for them, and re-layouts  109 us (15%)
  matrix products  90.4 us (13%)
  between operations  20.1 us (3%)
  starting transfers between devices  11.3 us (2%)
    another operation x30, other arithmetic, body(): diag_factor = jnp.linalg.cholesky(diag_block)  172 us
    psum x1, waiting for transfers between devices, broadcast(): return lax.psum(block, axis)  87.8 us
    another operation x3, other arithmetic, body(): lax.linalg.triangular_solve(diag_factor, row_block, left_side=False, lowe...  84 us
    all_gather x1, waiting for transfers between devices, body(): lax.all_gather(own_rows, 'row', axis=0, tiled=True)  72.5 us
    scatter x1, local copies, waits for them, and re-layouts, body(): slot_rows = jnp.zeros((device_count * capacity,), jnp.int32).at[targets.r...  60.3 us
    dot_general x1, matrix products, transposed_product(): lax.dot_general(left, right, (((1,), (1,)), ((), ())), precision=lax.Prec...  29.8 us
    another operation x24, local copies, waits for them, and re-layouts  24 us
    another operation x14, matrix products, body(): diag_factor = jnp.linalg.cholesky(diag_block)  23.2 us
  transfers between devices with their start and end apart: 5, of which 4 were waited for; matrix products, arithmetic and copies ran while one was open for 52% of the time, Pallas kernels for 0%

commit v1 on v0

v1 whole, which is shorter than its diff:
```python
import functools

import jax
import jax.numpy as jnp
from jax import lax
from jax.experimental import pallas as pl
from jax.experimental.pallas import tpu as pltpu
from jax.sharding import PartitionSpec as P

D = 512
PANEL = 1024
GROUP = 128
DATA_DEV = 1024
CAP = 4
N_ROW = 16
N_COL = 8
DEVICES = 128
RIDGE = 1.0
F32 = jnp.float32
BF = jnp.bfloat16
NT = (((1,), (1,)), ((), ()))
NN = (((1,), (0,)), ((), ()))
TN = (((0,), (0,)), ((), ()))


def dot(a, b, dims):
    return lax.dot_general(a, b, dims, preferred_element_type=F32)


def split(x):
    high = x.astype(BF)
    return high, (x - high.astype(F32)).astype(BF)


def dot3(a, b, dims):
    (ah, al), (bh, bl) = a, b
    return dot(ah, bh, dims) + (dot(ah, bl, dims) + dot(al, bh, dims))


def iota(shape, dim):
    return lax.broadcasted_iota(jnp.int32, shape, dim)


def sq_col(x):
    x = x.astype(F32)
    return jnp.sum(x * x, axis=1, keepdims=True)


def sq_row(x):
    x = x.astype(F32)
    high, low = split(x * x)
    ones = jnp.ones((8, x.shape[1]), BF)
    return (dot(ones, high, NT) + dot(ones, low, NT))[0:1]


def gram(left, right, left_sq, right_sq):
    return jnp.exp(-(left_sq + right_sq - 2.0 * dot(left, right, NT)) / D)


def send_kernel(where_ref, index_ref, desc_ref, out_ref):
    flat = where_ref[0]
    index = index_ref[...]
    match = lax.shift_right_logical(index, 10) == flat
    local = jnp.bitwise_and(index, DATA_DEV - 1).astype(F32)
    before = (iota((GROUP, GROUP), 0) < iota((GROUP, GROUP), 1)).astype(BF)
    rank = dot(match.astype(BF), before, NN)
    desc = desc_ref[...]
    rows = iota((DEVICES, DATA_DEV), 1).astype(F32)
    for k in range(CAP):
        slot = match & (rank == k)
        row = jnp.sum(jnp.where(slot, local, 0.0), axis=1, keepdims=True)
        pick = (rows == row).astype(BF)
        out_ref[:, k * D : (k + 1) * D] = dot(pick, desc, NN).astype(BF)


def take_group(index_row, arrived_ref, base):
    square = (GROUP, GROUP)
    shard_row = lax.shift_right_logical(index_row, 10).astype(F32)
    shard_row = jnp.broadcast_to(shard_row, square)
    eye = iota(square, 0) == iota(square, 1)
    shard_col = jnp.sum(jnp.where(eye, shard_row, 0.0), axis=1, keepdims=True)
    earlier = iota(square, 1) < iota(square, 0)
    rank = jnp.sum(
        jnp.where((shard_row == shard_col) & earlier, 1.0, 0.0), axis=1, keepdims=True
    )
    source = iota((GROUP, DEVICES), 1).astype(F32) == shard_col
    total = jnp.zeros((GROUP, D), F32)
    for k in range(CAP):
        pick = (source & (rank == k)).astype(BF)
        total = total + dot(pick, arrived_ref[:, (base + k) * D : (base + k + 1) * D], NN)
    return total.astype(BF)


def take_kernel(where_ref, index_ref, arrived_ref, out_ref):
    out_ref[0:GROUP] = take_group(index_ref[pl.ds(where_ref[0], 1), :], arrived_ref, 0)
    out_ref[GROUP:] = take_group(index_ref[pl.ds(where_ref[1], 1), :], arrived_ref, CAP)


def lane_b(x, c):
    return jnp.broadcast_to(x[:, c : c + 1], (8, 128))


def sub_b(x, j):
    return jnp.broadcast_to(x[j : j + 1, :], (8, 128))


def inverse_factor_128(x, sub):
    lane = iota((8, 128), 1)
    w = [(lane == sub + 8 * g).astype(F32) for g in range(16)]
    for t in range(16):
        first = 8 * t
        c = [lane_b(x[t], first + j) for j in range(8)]
        xt, wt = x[t], w[t]
        scale = jnp.zeros((8, 128), F32)
        rows = []
        for j in range(8):
            pivot = sub_b(c[j], j)
            over = 1.0 / pivot
            scale = jnp.where(sub == j, lax.rsqrt(pivot), scale)
            xj, wj = sub_b(xt, j), sub_b(wt, j)
            cj = [sub_b(c[q], j) for q in range(j + 1, 8)]
            rows.append((over, cj, xj, wj))
            if j < 7:
                m = jnp.where(sub > j, c[j] * over, 0.0)
                for q in range(j + 1, 8):
                    c[q] = c[q] - m * cj[q - j - 1]
                xt = xt - m * xj
                wt = wt - m * wj
        w[t] = wt * scale
        for g in range(t + 1, 16):
            xg, wg = x[g], w[g]
            c = [lane_b(xg, first + j) for j in range(8)]
            for j in range(8):
                over, cj, xj, wj = rows[j]
                m = c[j] * over
                for q in range(j + 1, 8):
                    c[q] = c[q] - m * cj[q - j - 1]
                xg = xg - m * xj
                wg = wg - m * wj
            x[g], w[g] = xg, wg
    return jnp.concatenate(w, 0)


def factor_kernel(panel_ref, high_ref, low_ref, x_ref):
    blocks = PANEL // 128
    panel = panel_ref[...]
    panel_row = sq_row(panel)
    panel_col = sq_col(panel)
    for i in range(blocks):
        s = slice(i * 128, i * 128 + 128)
        block = gram(panel[s], panel, panel_col[s], panel_row)
        eye = iota((128, PANEL), 1) == iota((128, PANEL), 0) + i * 128
        x_ref[s, :] = block + jnp.where(eye, RIDGE, 0.0)
    sub = iota((8, 128), 0)

    def step(k, _):
        k0 = pl.multiple_of(k * 128, 128)
        at_k = pl.ds(k0, 128)
        diag = x_ref[at_k, at_k]
        inverse = inverse_factor_128([diag[8 * g : 8 * g + 8] for g in range(16)], sub)
        x_ref[at_k, at_k] = jnp.where(iota((128, 128), 0) == iota((128, 128), 1), 1.0, 0.0)
        strip = dot3(split(inverse), split(x_ref[at_k, :]), NN)
        x_ref[at_k, :] = strip
        strip = split(strip)

        def update(i, _):
            at_i = pl.ds(pl.multiple_of(i * 128, 128), 128)
            left = split(x_ref[at_k, at_i])
            x_ref[at_i, at_k] = jnp.zeros((128, 128), F32)
            x_ref[at_i, :] -= dot3(left, strip, TN)
            return 0

        lax.fori_loop(k + 1, blocks, update, 0)
        return 0

    lax.fori_loop(0, blocks, step, 0)
    for i in range(blocks):
        s = slice(i * 128, i * 128 + 128)
        lower = iota((128, PANEL), 1) < (i + 1) * 128
        high, low = split(jnp.where(lower, x_ref[s, :], 0.0))
        high_ref[s, :] = high
        low_ref[s, :] = low


COL_TILE = 512
ROW_TILE = 256


def tile_kernel(
    where_ref, both_ref, col_ref, high_ref, low_ref, schur_ref, factor_ref, zh_ref, zl_ref
):
    my_row, my_col, owner = where_ref[0], where_ref[1], where_ref[2]
    panel = both_ref[PANEL:, :]
    panel_row = sq_row(panel)
    step = pl.program_id(0)

    @pl.when(step == 0)
    def _():
        for i in range(PANEL // ROW_TILE):
            s = slice(i * ROW_TILE, (i + 1) * ROW_TILE)
            rows = both_ref[s, :]
            block = gram(rows, panel, sq_col(rows), panel_row)
            eye = iota((ROW_TILE, PANEL), 1) == iota((ROW_TILE, PANEL), 0) + i * ROW_TILE
            block = block + jnp.where(eye & (my_row == owner), RIDGE, 0.0)
            inverse = (high_ref[...], low_ref[...])
            factor = dot3(split(block), inverse, NT)
            zh_ref[s, :], zl_ref[s, :] = split(dot3(split(factor), inverse, NN))
            share = jnp.zeros((ROW_TILE, GROUP), F32)
            for c in range(N_COL):
                share = jnp.where(my_col == c, factor[:, c * GROUP : (c + 1) * GROUP], share)
            factor_ref[s, :] = share

    cols = col_ref[...]
    at = iota((COL_TILE, PANEL), 0) + step * COL_TILE - owner * GROUP
    block = gram(cols, panel, sq_col(cols), panel_row)
    eye = (at >= 0) & (at < GROUP) & (iota((COL_TILE, PANEL), 1) == at + my_col * GROUP)
    block = split(block + jnp.where(eye, RIDGE, 0.0))
    cols_sq = sq_row(cols)
    for i in range(PANEL // ROW_TILE):
        s = slice(i * ROW_TILE, (i + 1) * ROW_TILE)
        rows = both_ref[s, :]
        tile = gram(rows, cols, sq_col(rows), cols_sq)
        shape = (ROW_TILE, COL_TILE)
        at = iota(shape, 1) + step * COL_TILE - my_row * GROUP
        eye = (at >= 0) & (at < GROUP) & (iota(shape, 0) + i * ROW_TILE == at + my_col * GROUP)
        tile = tile + jnp.where(eye, RIDGE, 0.0)
        schur_ref[s, :] = tile - dot3((zh_ref[s, :], zl_ref[s, :]), block, NT)


VMEM = pl.BlockSpec(memory_space=pltpu.VMEM)
SMEM = pl.BlockSpec(memory_space=pltpu.SMEM)


def call(kernel, out_shape, in_specs, scratch=(), **more):
    return pl.pallas_call(
        kernel,
        out_shape=out_shape,
        in_specs=in_specs,
        scratch_shapes=scratch,
        compiler_params=pltpu.CompilerParams(vmem_limit_bytes=56 << 20),
        **more,
    )


def body(descriptors, center_index, panel_index):
    my_row = lax.axis_index("row")
    my_col = lax.axis_index("col")
    owner = panel_index[0]
    flat = my_row * N_COL + my_col
    index = center_index.reshape(DEVICES, GROUP)
    sent = call(
        send_kernel, jax.ShapeDtypeStruct((DEVICES, CAP * D), BF), [SMEM, VMEM, VMEM]
    )(flat[None], index, descriptors)
    of_panel = lax.dynamic_slice_in_dim(sent, owner * N_COL, N_COL, 0)
    sent = jnp.concatenate([sent, jnp.tile(of_panel, (N_ROW, 1))], axis=1)
    arrived = lax.all_to_all(sent, ("row", "col"), 0, 0, tiled=True)
    mine = call(take_kernel, jax.ShapeDtypeStruct((2 * GROUP, D), BF), [SMEM, VMEM, VMEM])(
        jnp.stack([flat, owner * N_COL + my_col]), index, arrived
    )
    both = lax.all_gather(mine.reshape(2, GROUP, D), "col", axis=1)
    both = both.reshape(2 * PANEL, D)
    cols = lax.all_gather(mine[:GROUP], "row", axis=0, tiled=True)
    square = jax.ShapeDtypeStruct((PANEL, PANEL), BF)
    high, low = call(
        factor_kernel, (square, square), [VMEM], [pltpu.VMEM((PANEL, PANEL), F32)]
    )(both[PANEL:])
    width = N_ROW * GROUP
    schur, factor = call(
        tile_kernel,
        (
            jax.ShapeDtypeStruct((PANEL, width), F32),
            jax.ShapeDtypeStruct((PANEL, GROUP), F32),
        ),
        [SMEM, VMEM, pl.BlockSpec((COL_TILE, D), lambda i: (i, 0)), VMEM, VMEM],
        [pltpu.VMEM((PANEL, PANEL), BF), pltpu.VMEM((PANEL, PANEL), BF)],
        grid=(width // COL_TILE,),
        out_specs=(
            pl.BlockSpec((PANEL, COL_TILE), lambda i: (0, i)),
            pl.BlockSpec((PANEL, GROUP), lambda i: (0, 0)),
        ),
    )(jnp.stack([my_row, my_col, owner]), both, cols, high, low)
    return schur, factor


def solution(mesh):
    return jax.shard_map(
        body,
        mesh=mesh,
        in_specs=(P(("row", "col"), None), P(), P()),
        out_specs=(P("row", "col"), P("row", "col")),
        check_vma=False,
    )
```

time: 708 us -> 182 us (0.26)
  other arithmetic: 277 us -> 3.68 us
  waiting for transfers between devices: 193 us -> 37.6 us
  Pallas kernels: 0 us -> 104 us
  local copies, waits for them, and re-layouts: 109 us -> 9.88 us
  matrix products: 90.4 us -> 0 us
    another operation x33 -> x2, other arithmetic: 256 us -> 1.16 us  [the longest x1 0.58 us: body(): jnp.stack([my_row, my_col, owner])]
    pallas_call x0 -> x4, Pallas kernels: none -> 104 us  [the longest x1 53.4 us: body(): call(factor_kernel, (square, square), [VMEM], [pltpu.VMEM((PANEL, PANEL),...]
    psum x1 -> x0, waiting for transfers between devices: 87.8 us -> none  [broadcast(): return lax.psum(block, axis)]
    all_gather x3 -> x2, waiting for transfers between devices: 91.2 us -> 19.1 us  [the longest x1 19.1 us: body(): both = lax.all_gather(mine.reshape(2, GROUP, D), 'col', axis=1)]
    scatter x1 -> x0, local copies, waits for them, and re-layouts: 60.3 us -> none  [body(): slot_rows = jnp.zeros((device_count * capacity,), jnp.int32).at[targets.r...]
    dot_general x4 -> x0, matrix products: 45.3 us -> none  [the longest x1 29.8 us: transposed_product(): lax.dot_general(left, right, (((1,), (1,)), ((), ())), precision=lax.Prec...]
    another operation x29 -> x0, matrix products: 45.1 us -> none  [the longest x14 23.2 us: body(): diag_factor = jnp.linalg.cholesky(diag_block)]
    another operation x33 -> x1, local copies, waits for them, and re-layouts: 26.6 us -> 0.04 us  [body(): sent = jnp.concatenate([sent, jnp.tile(of_panel, (N_ROW, 1))], axis=1)]
  transfers between devices with their start and end apart: 5 -> 3, of which waited for: 4 -> 2; matrix products, arithmetic and copies ran while one was open for 52% -> 3% of each run, Pallas kernels for 0% -> 30%
where the time goes in v1:
time: 182 us; the launch traced here: 181 us
  Pallas kernels  104 us (57%)
  waiting for transfers between devices  37.6 us (21%)
  between operations  14.7 us (8%)
  starting transfers between devices  11.3 us (6%)
  local copies, waits for them, and re-layouts  9.88 us (5%)
  other arithmetic  3.68 us (2%)
    pallas_call x1, Pallas kernels, body(): call(factor_kernel, (square, square), [VMEM], [pltpu.VMEM((PANEL, PANEL),...  53.4 us
    pallas_call x1, Pallas kernels, body(): call(tile_kernel, (jax.ShapeDtypeStruct((PANEL, width), F32), jax.ShapeDt...  44.8 us
    all_gather x1, waiting for transfers between devices, body(): both = lax.all_gather(mine.reshape(2, GROUP, D), 'col', axis=1)  19.1 us
    all_to_all x1, waiting for transfers between devices, body(): arrived = lax.all_to_all(sent, ('row', 'col'), 0, 0, tiled=True)  18.5 us
    all_to_all x1, starting transfers between devices, body(): arrived = lax.all_to_all(sent, ('row', 'col'), 0, 0, tiled=True)  11.2 us
    unnamed x3, local copies, waits for them, and re-layouts  4.74 us
  transfers between devices with their start and end apart: 3, of which 2 were waited for; matrix products, arithmetic and copies ran while one was open for 3% of the time, Pallas kernels for 30%

profile of v1, /device:TPU:0, one launch (start us, length us, event | category | flops | bytes accessed | tf_op | source)
XLA Modules:
  0.0 180.8 jit_solution(8497334734673910836)
XLA Ops:
  7.8 3.0 %shard_map.50 = bf16[128,2048]{1,0:T(8,128)(2,1)} custom-call(s32[1]{0:T(128)} %bitcast.2.where_ref, s32[128,128]{1,0:T(8,128)} %bitcast.22, bf16[1024,512]{1,0:T(8,128)(2,1)} %desc_ref.1), custom_call_target="tpu_custom_call" | custom-call | tf_op jit(solution)/shard_map/pallas_call | solution.py:251
  10.8 0.8 constant_dynamic-slice_fusion
  11.6 1.1 maximum_bitcast_fusion
  12.7 0.5 broadcast.3
  13.2 1.4 reduce
  14.7 1.6 reshape.21
  16.2 11.2 %all-to-all-start = ((bf16[128,2,2048]{2,1,0:T(2,128)(2,1)}), bf16[128,2,2048]{2,1,0:T(2,128)(2,1)S(1)}, u32[]{:S(2)}, u32[]{:S(2)}) async-start(bf16[128,2,2048]{2,1,0:T(2,128)(2,1)} %reshape.21), calls=%async_computation | async-start | bytes 2097152 | tf_op jit(solution)/shard_map/all_to_all | solution.py:256
  27.4 0.0 all-gather.3.cloned.1.call-start
  27.5 0.6 pad_add_fusion.1.where_ref
  28.0 18.5 %all-to-all-done = bf16[128,2,2048]{2,1,0:T(2,128)(2,1)S(1)} async-done(((bf16[128,2,2048]{2,1,0:T(2,128)(2,1)}), bf16[128,2,2048]{2,1,0:T(2,128)(2,1)S(1)}, u32[]{:S(2)}, u32[]{:S(2)}) %all-to-all-start) | async-done | bytes 1048608 | tf_op jit(solution)/shard_map/all_to_all | solution.py:256
  46.5 1.0 reshape.22
  47.6 2.1 %copy.12 = bf16[128,1,4096]{2,0,1:T(8,128)(2,1)} copy(bf16[128,1,4096]{2,1,0:T(2,128)(2,1)S(1)} %reshape.22) | data formatting | bytes 2097152
  49.7 2.5 %shard_map.51 = bf16[256,512]{1,0:T(8,128)(2,1)} custom-call(s32[2]{0:T(128)} %pad_add_fusion.1.where_ref, s32[128,128]{1,0:T(8,128)} %bitcast.23, bf16[128,4096]{1,0:T(8,128)(2,1)} %bitcast.19), custom_call_target="tpu_custom_call" | custom-call | tf_op jit(solution)/shard_map/pallas_call | solution.py:257
  52.3 0.0 all-gather.3.cloned.1.call-update
  52.3 0.0 all-gather.5.cloned.1.call-start
  52.3 1.6 slice.12
  53.9 0.0 all-gather.5.cloned.1.call-update
  53.9 0.6 pad_add_fusion.where_ref
  54.5 19.1 %all-gather.3.cloned.1.call-done = bf16[2,8,128,512]{3,2,1,0:T(8,128)(2,1)} async-done(((bf16[2,1,128,512]{3,2,1,0:T(8,128)(2,1)}), bf16[2,8,128,512]{3,2,1,0:T(8,128)(2,1)}) %all-gather.3.cloned.1.call-update) | async-done | bytes 2097168 | tf_op jit(solution)/shard_map/all_gather | solution.py:260
  73.5 2.3 %slice.13 = bf16[1,8,128,512]{3,2,1,0:T(8,128)(2,1)} slice(bf16[2,8,128,512]{3,2,1,0:T(8,128)(2,1)} %all-gather.3.cloned.1.call-done), slice={[1:2], [0:8], [0:128], [0:512]} | slice | bytes 2097152 | tf_op jit(solution)/shard_map/slice | solution.py:266
  75.8 53.4 %shard_map.52 = (bf16[1024,1024]{1,0:T(8,128)(2,1)}, bf16[1024,1024]{1,0:T(8,128)(2,1)}) custom-call(bf16[1024,512]{1,0:T(8,128)(2,1)} %bitcast.20), custom_call_target="tpu_custom_call" | custom-call | tf_op jit(solution)/shard_map/pallas_call | solution.py:264
  129.2 0.0 all-gather.5.cloned.1.call-done.col_ref
  129.2 44.8 %shard_map.53 = (f32[1024,2048]{1,0:T(8,128)}, f32[1024,128]{1,0:T(8,128)}) custom-call(s32[3]{0:T(128)} %pad_add_fusion.where_ref, bf16[2048,512]{1,0:T(8,128)(2,1)} %bitcast.18, bf16[2048,512]{1,0:T(8,128)(2,1)} %all-gather.5.cloned.1.call-done.col_ref, bf16[1024,1024]{1,0:T(8,128)(2,1)} %get-tuple-element.4.high_ref, ...), custom_call_target="tpu_custom_call" | custom-call | tf_op jit(solution)/shard_map/pallas_call | solution.py:268
  (1 shorter events, 0.0 us)
Async XLA Ops:
  16.2 30.3 %all-to-all-start = ((bf16[128,2,2048]{2,1,0:T(2,128)(2,1)}), bf16[128,2,2048]{2,1,0:T(2,128)(2,1)S(1)}, u32[]{:S(2)}, u32[]{:S(2)}) async-start(bf16[128,2,2048]{2,1,0:T(2,128)(2,1)} %reshape.21), calls=%async_computation | async-start | bytes 2097152 | tf_op jit(solution)/shard_map/all_to_all | solution.py:256
  27.4 46.1 %all-gather.3.cloned.1.call-start = ((), (), s32[]{:S(2)}) async-start(), calls=%async_computation.1 | async-start | bytes 2359296 | tf_op jit(solution)/shard_map/all_gather | solution.py:260
  52.3 76.9 %all-gather.5.cloned.1.call-start = ((), (), s32[]{:S(2)}) async-start(), calls=%async_computation.2 | async-start | bytes 2228224 | tf_op jit(solution)/shard_map/all_gather | solution.py:262
Sparse Core Ops, SparseCore 0:
  52.4 21.1 all-gather.2
  75.7 45.5 all-gather.4

commit v2 on v1

v2 whole, which is shorter than its diff:
```python
import functools

import jax
import jax.numpy as jnp
from jax import lax
from jax.experimental import pallas as pl
from jax.experimental.pallas import tpu as pltpu
from jax.sharding import PartitionSpec as P

D = 512
PANEL = 1024
GROUP = 128
DATA_DEV = 1024
CAP = 4
N_ROW = 16
N_COL = 8
DEVICES = 128
RIDGE = 1.0
SLOTS = 2 * CAP
F32 = jnp.float32
BF = jnp.bfloat16
NT = (((1,), (1,)), ((), ()))
NN = (((1,), (0,)), ((), ()))
TN = (((0,), (0,)), ((), ()))


def dot(a, b, dims):
    return lax.dot_general(a, b, dims, preferred_element_type=F32)


def split(x):
    high = x.astype(BF)
    return high, (x - high.astype(F32)).astype(BF)


def dot3(a, b, dims):
    (ah, al), (bh, bl) = a, b
    return dot(ah, bh, dims) + (dot(ah, bl, dims) + dot(al, bh, dims))


def iota(shape, dim):
    return lax.broadcasted_iota(jnp.int32, shape, dim)


K_EXP = 1.4426950408889634 / D


def squares(x):
    x = x.astype(F32)
    return split(x * x)


def sq_col(x):
    high, low = squares(x)
    ones = jnp.ones((x.shape[1], 128), BF)
    return (dot(high, ones, NN) + dot(low, ones, NN)) * K_EXP


def sq_row(x):
    high, low = squares(x)
    ones = jnp.ones((8, x.shape[1]), BF)
    return (dot(ones, high, NT) + dot(ones, low, NT))[0:1] * K_EXP


def widen(x, width):
    return jnp.concatenate([x] * (width // 128), 1)


def gram(left, right, left_sq, right_sq):
    inner = dot(left, right, NT)
    return jnp.exp2((inner * (2.0 * K_EXP) - widen(left_sq, right.shape[0])) - right_sq)


def send_kernel(where_ref, index_ref, desc_ref, out_ref):
    flat, first = where_ref[0], where_ref[1]
    square = (GROUP, GROUP)
    index = index_ref[...]
    match = lax.shift_right_logical(index, 10) == flat
    local = jnp.bitwise_and(index, DATA_DEV - 1).astype(F32)
    before = (iota(square, 0) < iota(square, 1)).astype(BF)
    rank = dot(match.astype(BF), before, NN)
    lane = iota(square, 1)
    own = jnp.zeros(square, F32)
    panel = jnp.zeros(square, F32)
    for k in range(CAP):
        slot = match & (rank == k)
        row = jnp.sum(jnp.where(slot, local, 0.0), axis=1, keepdims=True)
        own = jnp.where(lane == k, row, own)
        panel = jnp.where(lane == k + CAP, row, panel)
    pick = (lane == first + jnp.bitwise_and(iota(square, 0), N_COL - 1)).astype(BF)
    high, low = split(panel)
    high, low = split(own + (dot(pick, high, NN) + dot(pick, low, NN)))
    desc = desc_ref[...]
    step = 256
    for i in range(0, DEVICES * SLOTS, step):
        at = iota((step, DEVICES), 0) + i
        pick = (iota((step, DEVICES), 1) == lax.shift_right_logical(at, 3)).astype(BF)
        rows = dot(pick, high, NN) + dot(pick, low, NN)
        mine = iota((step, DEVICES), 1) == jnp.bitwise_and(at, SLOTS - 1)
        row = jnp.sum(jnp.where(mine, rows, 0.0), axis=1, keepdims=True)
        pick = (iota((step, DATA_DEV), 1).astype(F32) == row).astype(BF)
        out_ref[i : i + step] = dot(pick, desc, NN).astype(BF)


def take_group(index_row, arrived, base):
    square = (GROUP, GROUP)
    shard_row = lax.shift_right_logical(index_row, 10).astype(F32)
    shard_row = jnp.broadcast_to(shard_row, square)
    eye = iota(square, 0) == iota(square, 1)
    shard_col = jnp.sum(jnp.where(eye, shard_row, 0.0), axis=1, keepdims=True)
    earlier = iota(square, 1) < iota(square, 0)
    rank = jnp.sum(
        jnp.where((shard_row == shard_col) & earlier, 1.0, 0.0), axis=1, keepdims=True
    )
    at = shard_col * SLOTS + rank + base
    pick = (iota((GROUP, DEVICES * SLOTS), 1).astype(F32) == at).astype(BF)
    return dot(pick, arrived, NN).astype(BF)


def take_kernel(where_ref, index_ref, arrived_ref, both_ref, own_ref):
    flat, first, my_col = where_ref[0], where_ref[1], where_ref[2]
    arrived = arrived_ref[...]
    own = take_group(index_ref[pl.ds(flat, 1), :], arrived, 0)
    both_ref[0] = own
    own_ref[...] = own
    both_ref[1] = take_group(index_ref[pl.ds(first + my_col, 1), :], arrived, CAP)


def lane_b(x, c):
    return jnp.broadcast_to(x[:, c : c + 1], (8, 128))


def sub_b(x, j):
    return jnp.broadcast_to(x[j : j + 1, :], (8, 128))


def tree(terms):
    while len(terms) > 1:
        pairs = [terms[i] + terms[i + 1] for i in range(0, len(terms) - 1, 2)]
        terms = pairs + terms[len(terms) & ~1 :]
    return terms[0]


def far_update(x, w, solved, t):
    pad = jnp.zeros((8, 256), F32)
    rows = jnp.concatenate([solved, pad] if t % 2 == 0 else [pad, solved], 0)
    k = t // 2

    def place(part):
        above = [jnp.zeros((16 * k, 256), BF)] if k else []
        below = [jnp.zeros((112 - 16 * k, 256), BF)] if k < 7 else []
        return jnp.concatenate(above + [part] + below, 0)

    high, low = split(rows)
    far = jnp.concatenate(x[t + 2 :], 0)
    change = dot3(split(far), (place(high), place(low)), NN)
    for i, g in enumerate(range(t + 2, 16)):
        part = change[8 * i : 8 * i + 8]
        x[g] = x[g] - part[:, :128]
        w[g] = w[g] - part[:, 128:]


def inverse_factor_128(x, sub):
    lane = iota((8, 128), 1)
    w = [(lane == sub + 8 * g).astype(F32) for g in range(16)]
    c = [lane_b(x[0], j) for j in range(8)]
    solved = None
    for t in range(16):
        last = t == 15
        if 0 < t < 15:
            far_update(x, w, solved, t - 1)
        ahead = [] if last else [lane_b(x[t], 8 * t + 8 + q) for q in range(8)]
        xt, wt = x[t], w[t]
        out = wt
        for j in range(0, 8, 2):
            p, q, r = sub_b(c[j], j), sub_b(c[j + 1], j), sub_b(c[j + 1], j + 1)
            det = p * r - q * q
            over = 1.0 / det
            root = lax.rsqrt(p)
            over_p = root * root
            at0, at1 = sub == j, sub == j + 1
            m0 = jnp.where(at0, -1.0, jnp.where(at1, 0.0, c[j]))
            m1 = jnp.where(at1, -1.0, jnp.where(at0, 0.0, c[j + 1]))
            k0 = (m0 * r - m1 * q) * over
            k1 = (m1 * p - m0 * q) * over
            keep = jnp.logical_not(at0 | at1)

            def eliminate(v):
                return jnp.where(keep, v, 0.0) - (k0 * sub_b(v, j) + k1 * sub_b(v, j + 1))

            w0, w1 = sub_b(wt, j), sub_b(wt, j + 1)
            out = jnp.where(at0, w0 * root, out)
            out = jnp.where(at1, (w1 - (q * over_p) * w0) * lax.rsqrt(det * over_p), out)
            for i in range(j + 2, 8):
                c[i] = eliminate(c[i])
            if not last:
                ahead = [eliminate(v) for v in ahead]
                xt = eliminate(xt)
            if not last or j < 6:
                wt = eliminate(wt)
        w[t] = out
        if last:
            break
        solved = jnp.concatenate([xt, wt], 1)
        g = t + 1
        m = [lane_b(x[g], 8 * t + j) for j in range(8)]
        c = [
            lane_b(x[g], 8 * g + q) - tree([m[j] * sub_b(ahead[q], j) for j in range(8)])
            for q in range(8)
        ]
        x[g] = x[g] - tree([m[j] * sub_b(xt, j) for j in range(8)])
        w[g] = w[g] - tree([m[j] * sub_b(wt, j) for j in range(8)])
    return jnp.concatenate(w, 0)


def factor_kernel(panel_ref, high_ref, low_ref, x_ref):
    blocks = PANEL // 128
    panel = panel_ref[...].reshape(PANEL, D)
    panel_row = sq_row(panel)
    panel_col = sq_col(panel)
    for i in range(blocks):
        s = slice(i * 128, i * 128 + 128)
        block = gram(panel[s], panel, panel_col[s], panel_row)
        eye = iota((128, PANEL), 1) == iota((128, PANEL), 0) + i * 128
        x_ref[s, :] = block + jnp.where(eye, RIDGE, 0.0)
    sub = iota((8, 128), 0)

    def step(k, _):
        k0 = pl.multiple_of(k * 128, 128)
        at_k = pl.ds(k0, 128)
        diag = x_ref[at_k, at_k]
        inverse = inverse_factor_128([diag[8 * g : 8 * g + 8] for g in range(16)], sub)
        x_ref[at_k, at_k] = jnp.where(iota((128, 128), 0) == iota((128, 128), 1), 1.0, 0.0)
        strip = dot3(split(inverse), split(x_ref[at_k, :]), NN)
        x_ref[at_k, :] = strip
        strip = split(strip)

        def update(i, _):
            at_i = pl.ds(pl.multiple_of(i * 128, 128), 128)
            left = split(x_ref[at_k, at_i])
            x_ref[at_i, at_k] = jnp.zeros((128, 128), F32)
            x_ref[at_i, :] -= dot3(left, strip, TN)
            return 0

        lax.fori_loop(k + 1, blocks, update, 0)
        return 0

    lax.fori_loop(0, blocks, step, 0)
    for i in range(blocks):
        s = slice(i * 128, i * 128 + 128)
        lower = iota((128, PANEL), 1) < (i + 1) * 128
        high, low = split(jnp.where(lower, x_ref[s, :], 0.0))
        high_ref[s, :] = high
        low_ref[s, :] = low


COL_TILE = 256
ROW_TILE = 512
BLOCK = 256


def tile_kernel(
    where_ref, both_ref, col_ref, high_ref, low_ref, schur_ref, factor_ref,
    gh_ref, gl_ref, zh_ref, zl_ref, row_sq_ref, panel_sq_ref
):
    my_row, my_col, owner = where_ref[0], where_ref[1], where_ref[2]
    panel = both_ref[:, 1].reshape(PANEL, D)
    step = pl.program_id(0)

    @pl.when(step == 0)
    def _():
        panel_sq_ref[...] = jnp.broadcast_to(sq_row(panel), (8, PANEL))

        def rows_part(h, _):
            h0 = pl.multiple_of(h * ROW_TILE, ROW_TILE)
            at = pl.ds(h0, ROW_TILE)
            per = ROW_TILE // GROUP
            rows = both_ref[pl.ds(h * per, per), 0].reshape(ROW_TILE, D)
            rows_sq = sq_col(rows)
            row_sq_ref[at, :] = rows_sq
            ridge = jnp.where(my_row == owner, RIDGE, 0.0)
            shape = (ROW_TILE, BLOCK)
            for b in range(PANEL // BLOCK):
                s = slice(b * BLOCK, (b + 1) * BLOCK)
                block = gram(rows, panel[s], rows_sq, panel_sq_ref[0:1, s])
                eye = iota(shape, 1) + b * BLOCK == iota(shape, 0) + h0
                block = block + jnp.where(eye, ridge, 0.0)
                gh_ref[at, s], gl_ref[at, s] = split(block)
            share = jnp.zeros((ROW_TILE, GROUP), F32)
            for b in range(PANEL // BLOCK):
                s, upto = slice(b * BLOCK, (b + 1) * BLOCK), slice(0, (b + 1) * BLOCK)
                factor = dot3(
                    (gh_ref[at, upto], gl_ref[at, upto]),
                    (high_ref[s, upto], low_ref[s, upto]),
                    NT,
                )
                zh_ref[at, s], zl_ref[at, s] = split(factor)
                share = jnp.where(my_col == 2 * b, factor[:, :GROUP], share)
                share = jnp.where(my_col == 2 * b + 1, factor[:, GROUP:], share)
            factor_ref[at, :] = share
            for b in range(PANEL // BLOCK):
                s, upon = slice(b * BLOCK, (b + 1) * BLOCK), slice(b * BLOCK, PANEL)
                zh_ref[at, s], zl_ref[at, s] = split(
                    dot3(
                        (zh_ref[at, upon], zl_ref[at, upon]),
                        (high_ref[upon, s], low_ref[upon, s]),
                        NN,
                    )
                )
            return 0

        lax.fori_loop(0, PANEL // ROW_TILE, rows_part, 0)

    cols = col_ref[...]
    block = split(gram(cols, panel, sq_col(cols), panel_sq_ref[0:1, :]))
    cols_sq = sq_row(cols)
    for h in range(PANEL // ROW_TILE):
        s = slice(h * ROW_TILE, (h + 1) * ROW_TILE)
        per = ROW_TILE // GROUP
        rows = both_ref[h * per : (h + 1) * per, 0].reshape(ROW_TILE, D)
        tile = gram(rows, cols, row_sq_ref[s, :], cols_sq)
        schur_ref[s, :] = tile - dot3((zh_ref[s, :], zl_ref[s, :]), block, NT)

    @pl.when(step == owner // 2)
    def _():
        at = pl.ds(pl.multiple_of((owner % 2) * GROUP, GROUP), GROUP)
        of = pl.ds(pl.multiple_of(my_col * GROUP, GROUP), GROUP)
        z = zh_ref[:, of].astype(F32) + zl_ref[:, of].astype(F32)
        schur_ref[:, at] = schur_ref[:, at] - RIDGE * z

    @pl.when(step == my_row // 2)
    def _():
        at = pl.ds(pl.multiple_of((my_row % 2) * GROUP, GROUP), GROUP)
        of = pl.ds(pl.multiple_of(my_col * GROUP, GROUP), GROUP)
        eye = iota((GROUP, GROUP), 0) == iota((GROUP, GROUP), 1)
        schur_ref[of, at] = schur_ref[of, at] + jnp.where(eye, RIDGE, 0.0)


VMEM = pl.BlockSpec(memory_space=pltpu.VMEM)
SMEM = pl.BlockSpec(memory_space=pltpu.SMEM)


def call(kernel, out_shape, in_specs, scratch=(), **more):
    return pl.pallas_call(
        kernel,
        out_shape=out_shape,
        in_specs=in_specs,
        scratch_shapes=scratch,
        compiler_params=pltpu.CompilerParams(vmem_limit_bytes=56 << 20),
        **more,
    )


def body(descriptors, center_index, panel_index):
    my_row = lax.axis_index("row")
    my_col = lax.axis_index("col")
    owner = panel_index[0]
    flat = my_row * N_COL + my_col
    where = jnp.stack([flat, owner * N_COL, my_col, my_row, owner])
    index = center_index.reshape(DEVICES, GROUP)
    sent = call(
        send_kernel, jax.ShapeDtypeStruct((DEVICES * SLOTS, D), BF), [SMEM, VMEM, VMEM]
    )(where, index, descriptors)
    arrived = lax.all_to_all(sent, ("row", "col"), 0, 0, tiled=True)
    mine, own = call(
        take_kernel,
        (jax.ShapeDtypeStruct((2, GROUP, D), BF), jax.ShapeDtypeStruct((GROUP, D), BF)),
        [SMEM, VMEM, VMEM],
    )(where, index, arrived)
    both = lax.all_gather(mine, "col", axis=0)
    cols = lax.all_gather(own, "row", axis=0, tiled=True)
    square = jax.ShapeDtypeStruct((PANEL, PANEL), BF)
    high, low = call(
        factor_kernel,
        (square, square),
        [pl.BlockSpec((N_COL, 1, GROUP, D), lambda i: (0, 1, 0, 0))],
        [pltpu.VMEM((PANEL, PANEL), F32)],
        grid=(1,),
        out_specs=(pl.BlockSpec((PANEL, PANEL), lambda i: (0, 0)),) * 2,
    )(both)
    width = N_ROW * GROUP
    half = pltpu.VMEM((PANEL, PANEL), BF)
    schur, factor = call(
        tile_kernel,
        (
            jax.ShapeDtypeStruct((PANEL, width), F32),
            jax.ShapeDtypeStruct((PANEL, GROUP), F32),
        ),
        [SMEM, VMEM, pl.BlockSpec((COL_TILE, D), lambda i: (i, 0)), VMEM, VMEM],
        [half, half, half, half, pltpu.VMEM((PANEL, 128), F32), pltpu.VMEM((8, PANEL), F32)],
        grid=(width // COL_TILE,),
        out_specs=(
            pl.BlockSpec((PANEL, COL_TILE), lambda i: (0, i)),
            pl.BlockSpec((PANEL, GROUP), lambda i: (0, 0)),
        ),
    )(jnp.stack([my_row, my_col, owner]), both, cols, high, low)
    return schur, factor


def solution(mesh):
    return jax.shard_map(
        body,
        mesh=mesh,
        in_specs=(P(("row", "col"), None), P(), P()),
        out_specs=(P("row", "col"), P("row", "col")),
        check_vma=False,
    )
```

time: 182 us -> 162 us (0.89)
  blocking collectives: 0 us -> 30.4 us
  Pallas kernels: 104 us -> 89.2 us
  waiting for transfers between devices: 37.6 us -> 25.8 us
  starting transfers between devices: 11.3 us -> 0.08 us
  local copies, waits for them, and re-layouts: 9.88 us -> 0.66 us
  other arithmetic: 3.68 us -> 0.65 us
    all_to_all x0 -> x1, blocking collectives: none -> 30.4 us  [body(): arrived = lax.all_to_all(sent, ('row', 'col'), 0, 0, tiled=True)]
    all_to_all x1 -> x0, waiting for transfers between devices: 18.5 us -> none  [body(): arrived = lax.all_to_all(sent, ('row', 'col'), 0, 0, tiled=True)]
    all_to_all x1 -> x0, starting transfers between devices: 11.2 us -> none  [body(): arrived = lax.all_to_all(sent, ('row', 'col'), 0, 0, tiled=True)]
    pallas_call x3, Pallas kernels: 58.9 us -> 50.6 us  [the longest x1 43.2 us: body(): call(factor_kernel, (square, square), [pl.BlockSpec((N_COL, 1, GROUP, D),...]
    pallas_call x1, Pallas kernels: 44.8 us -> 38.5 us  [body(): call(tile_kernel, (jax.ShapeDtypeStruct((PANEL, width), F32), jax.ShapeDt...]
    all_gather x2, waiting for transfers between devices: 19.1 us -> 25.1 us  [the longest x1 19.9 us: body(): both = lax.all_gather(mine, 'col', axis=0)]
    unnamed x3 -> x0, local copies, waits for them, and re-layouts: 4.74 us -> none
    slice x2 -> x0, local copies, waits for them, and re-layouts: 3.82 us -> none  [the longest x1 2.26 us: body(): both[PANEL:]]
  transfers between devices with their start and end apart: 3 -> 2, of which waited for: 2 -> 2; matrix products, arithmetic and copies ran while one was open for 3% -> 0% of each run, Pallas kernels for 30% -> 27%
where the time goes in v2:
time: 162 us; the launch traced here: 161 us
  Pallas kernels  89.2 us (55%)
  blocking collectives  30.4 us (19%)
  waiting for transfers between devices  25.8 us (16%)
  between operations  14.7 us (9%)
    pallas_call x1, Pallas kernels, body(): call(factor_kernel, (square, square), [pl.BlockSpec((N_COL, 1, GROUP, D),...  43.2 us
    pallas_call x1, Pallas kernels, body(): call(tile_kernel, (jax.ShapeDtypeStruct((PANEL, width), F32), jax.ShapeDt...  38.5 us
    all_to_all x1, blocking collectives, body(): arrived = lax.all_to_all(sent, ('row', 'col'), 0, 0, tiled=True)  30.4 us
    all_gather x1, waiting for transfers between devices, body(): both = lax.all_gather(mine, 'col', axis=0)  19.9 us
    all_gather x1, waiting for transfers between devices, body(): cols = lax.all_gather(own, 'row', axis=0, tiled=True)  5.22 us
    pallas_call x1, Pallas kernels, body(): call(send_kernel, jax.ShapeDtypeStruct((DEVICES * SLOTS, D), BF), [SMEM,...  4.9 us
  transfers between devices with their start and end apart: 2, of which 2 were waited for; matrix products, arithmetic and copies ran while one was open for 0% of the time, Pallas kernels for 27%

profile of v2, /device:TPU:0, one launch (start us, length us, event | category | flops | bytes accessed | tf_op | source)
XLA Modules:
  0.0 161.4 jit_solution(11676699010850137867)
XLA Ops:
  7.2 0.0 all-gather.6.cloned.1.call-start
  7.9 0.7 stack.22.where_ref
  8.5 4.9 %shard_map.50 = bf16[1024,512]{1,0:T(8,128)(2,1)} custom-call(s32[5]{0:T(128)} %stack.22.where_ref, s32[128,128]{1,0:T(8,128)} %bitcast.11, bf16[1024,512]{1,0:T(8,128)(2,1)} %desc_ref.1), custom_call_target="tpu_custom_call" | custom-call | tf_op jit(solution)/shard_map/pallas_call | solution.py:361
  13.4 30.4 %all_to_all.11 = bf16[128,8,512]{2,1,0:T(8,128)(2,1)} all-to-all(bf16[128,8,512]{2,1,0:T(8,128)(2,1)} %bitcast.9), channel_id=1, replica_groups=mesh['row'=16,'col'=8] {'row','col'}, dimensions={0} | all-to-all | bytes 2097152 | tf_op jit(solution)/shard_map/all_to_all | solution.py:364
  43.8 2.6 %shard_map.51 = (bf16[2,128,512]{2,1,0:T(8,128)(2,1)}, bf16[128,512]{1,0:T(8,128)(2,1)}) custom-call(s32[5]{0:T(128)} %stack.22.where_ref, s32[128,128]{1,0:T(8,128)} %bitcast.12, bf16[1024,512]{1,0:T(8,128)(2,1)} %bitcast.10), custom_call_target="tpu_custom_call" | custom-call | tf_op jit(solution)/shard_map/pallas_call | solution.py:365
  46.4 0.0 all-gather.6.cloned.1.call-update
  46.4 0.0 all-gather.4.cloned.1.call-start
  46.5 0.7 all-gather.4.cloned.1.call-update
  47.2 0.7 pad_add_fusion.where_ref
  47.8 19.9 %all-gather.6.cloned.1.call-done = bf16[16,128,512]{2,1,0:T(8,128)(2,1)} async-done(((bf16[2,128,512]{2,1,0:T(8,128)(2,1)}), bf16[16,128,512]{2,1,0:T(8,128)(2,1)}) %all-gather.6.cloned.1.call-update) | async-done | bytes 2097168 | tf_op jit(solution)/shard_map/all_gather | solution.py:370
  67.7 43.2 %shard_map.52 = (bf16[1024,1024]{1,0:T(8,128)(2,1)}, bf16[1024,1024]{1,0:T(8,128)(2,1)}) custom-call(bf16[8,2,128,512]{3,2,1,0:T(8,128)(2,1)} %bitcast.7), custom_call_target="tpu_custom_call" | custom-call | tf_op jit(solution)/shard_map/pallas_call | solution.py:373
  110.9 5.2 %all-gather.4.cloned.1.call-done.col_ref = bf16[2048,512]{1,0:T(8,128)(2,1)} async-done(((bf16[128,512]{1,0:T(8,128)(2,1)}), bf16[2048,512]{1,0:T(8,128)(2,1)}) %all-gather.4.cloned.1.call-update) | async-done | bytes 2097168 | tf_op jit(solution)/shard_map/all_gather | solution.py:371
  116.1 38.5 %shard_map.53 = (f32[1024,2048]{1,0:T(8,128)}, f32[1024,128]{1,0:T(8,128)}) custom-call(s32[3]{0:T(128)} %pad_add_fusion.where_ref, bf16[8,2,128,512]{3,2,1,0:T(8,128)(2,1)} %bitcast.8, bf16[2048,512]{1,0:T(8,128)(2,1)} %all-gather.4.cloned.1.call-done.col_ref, bf16[1024,1024]{1,0:T(8,128)(2,1)} %get-tuple-element.8.high_ref, ...), custom_call_target="tpu_custom_call" | custom-call | tf_op jit(solution)/shard_map/pallas_call | solution.py:383
Async XLA Ops:
  7.2 60.5 %all-gather.6.cloned.1.call-start = ((), (), s32[]{:S(2)}) async-start(), calls=%async_computation.2 | async-start | bytes 2359296 | tf_op jit(solution)/shard_map/all_gather | solution.py:370
  46.4 69.6 %all-gather.4.cloned.1.call-start = ((), (), s32[]{:S(2)}) async-start(), calls=%async_computation.1 | async-start | bytes 2228224 | tf_op jit(solution)/shard_map/all_gather | solution.py:371
Sparse Core Ops, SparseCore 0:
  46.6 21.0 all-gather.5
  70.4 45.6 all-gather.3
